TPU v7x, 128 devices: a whole 4x4x4 slice. The times are simulated.
128 devices in a mesh: tile: 64 (over z, x, y_lo, core), chan: 2 (over y_hi).
Axes of the slice: x: 4, y: 4 (y_hi: 2, y_lo: 2; y = y_hi * 2 + y_lo), z: 4, core: 2. Of those that a mesh axis runs over, the one named last changes fastest.
Arguments:
- inputs: bfloat16 [128, 64, 4096], P('tile', 'chan'), may hold values from -6 to 6
- gluing: int32 [128, 4, 3], P('tile'), may hold values from 0 to 127, as said below
- conv_weight: bfloat16 [64, 64, 3, 3], replicated, may hold values from -0.25 to 0.25
- level_weight: bfloat16 [128, 64, 2, 2], replicated, may hold values from -0.375 to 0.375
- cotangent: bfloat16 [128, 128, 1024], P('tile', 'chan'), may hold values from -6 to 6
Outputs:
- level: bfloat16 [128, 128, 1024], P('tile', 'chan')
- grad_inputs: bfloat16 [128, 64, 4096], P('tile', 'chan')
- grad_conv: float32 [64, 64, 3, 3], P(None, 'chan')
- grad_level: float32 [128, 64, 2, 2], P(None, 'chan')
Inputs may be any that keep to these rules, and one draw needn't show every extreme that they name: Entry [t, s] = (u, r, f) with r in 0..3 and f in 0..1 says that side s of tile t is glued to side r of tile u; the gluing is symmetric: entry [u, r] is (t, s, f), and no side is glued to itself.
All inputs are finite; a program needn't handle non-finite values.
Results may differ from a plain program's by a relative error of at most 0.005.
Values may be sent and summed in bfloat16 or wider, within the bound.
No kernel may reach another device: no remote copies, remote signals or barrier semaphores. Data moves between devices by JAX's collectives and lax.ppermute only.
A program may use at most 128 MiB of HBM per device.

v0:
```python
import jax
import jax.numpy as jnp
from jax import lax
from jax.sharding import PartitionSpec as P

S = 64


def edge_strips(source):
    return jnp.stack(
        [source[:, :, 0, :], source[:, :, -1, :], source[:, :, :, 0], source[:, :, :, -1]], axis=1
    )


def border_strips(padded):
    return jnp.stack(
        [
            padded[:, :, 0, 1:-1],
            padded[:, :, -1, 1:-1],
            padded[:, :, 1:-1, 0],
            padded[:, :, 1:-1, -1],
        ],
        axis=1,
    )


def orient(strips, gluing):
    return jnp.where(gluing[:, :, 2][:, :, None, None] == 1, strips[..., ::-1], strips)


def make_picker(gluing):
    target = gluing[:, :, 0] * 4 + gluing[:, :, 1]

    def picker(current, received, first_row):
        strip_count = received.shape[0] * 4
        received_rows = received.reshape((strip_count,) + received.shape[2:])
        inside = (target >= 0) & (target < strip_count)
        chosen = jnp.take(received_rows, jnp.clip(target, 0, strip_count - 1), axis=0)
        return jnp.where(inside[:, :, None, None], chosen, current)

    return picker


def assemble(source, halo_cells):
    tile_count, chan_count = (source.shape[0], source.shape[1])
    corner = jnp.zeros((tile_count, chan_count, 1), source.dtype)
    top_row = jnp.concatenate([corner, halo_cells[:, 0], corner], axis=2)[:, :, None, :]
    low_row = jnp.concatenate([corner, halo_cells[:, 1], corner], axis=2)[:, :, None, :]
    middle = jnp.concatenate(
        [halo_cells[:, 2][:, :, :, None], source, halo_cells[:, 3][:, :, :, None]], axis=3
    )
    return jnp.concatenate([top_row, middle, low_row], axis=2)


def conv_three(padded, weight):
    extent = padded.shape[2] - 2
    summed = None
    for row_tap in range(3):
        for col_tap in range(3):
            product_term = jnp.einsum(
                "oc,ncxy->noxy",
                weight[:, :, row_tap, col_tap],
                padded[:, :, row_tap : row_tap + extent, col_tap : col_tap + extent],
                preferred_element_type=jnp.float32,
            )
            summed = product_term if summed is None else summed + product_term
    return summed


def conv_two(hidden, weight):
    tile_count, chan_count, extent = (hidden.shape[0], hidden.shape[1], hidden.shape[2])
    summed = None
    for row_tap in range(2):
        for col_tap in range(2):
            sampled = hidden[:, :, row_tap::2, col_tap::2].reshape(tile_count, chan_count, -1)
            product_term = jnp.einsum(
                "oc,ncp->nop",
                weight[:, :, row_tap, col_tap],
                sampled,
                preferred_element_type=jnp.float32,
            )
            summed = product_term if summed is None else summed + product_term
    return summed.reshape(tile_count, weight.shape[0], extent // 2, extent // 2)


def level_grads(hidden, cot_full, weight):
    tile_count, chan_count, extent = (hidden.shape[0], hidden.shape[1], hidden.shape[2])
    half = extent // 2
    cot_rows = cot_full.reshape(tile_count, cot_full.shape[1], -1)
    weight_rows = []
    spread_rows = []
    for row_tap in range(2):
        weight_cols = []
        spread_cols = []
        for col_tap in range(2):
            sampled = hidden[:, :, row_tap::2, col_tap::2].reshape(tile_count, chan_count, -1)
            weight_cols.append(
                jnp.einsum("nop,ncp->oc", cot_rows, sampled, preferred_element_type=jnp.float32)
            )
            spread = jnp.einsum(
                "oc,nop->ncp",
                weight[:, :, row_tap, col_tap],
                cot_rows,
                preferred_element_type=jnp.float32,
            )
            spread_cols.append(spread.reshape(tile_count, chan_count, half, half))
        weight_rows.append(jnp.stack(weight_cols, axis=-1))
        spread_rows.append(jnp.stack(spread_cols, axis=-1))
    grad_weight = jnp.stack(weight_rows, axis=2)
    grad_hidden = jnp.stack(spread_rows, axis=3).reshape(tile_count, chan_count, extent, extent)
    return (grad_weight, grad_hidden)


def conv_grads(padded, grad_full, weight):
    extent = padded.shape[2] - 2
    grad_padded = jnp.zeros(padded.shape, jnp.float32)
    weight_rows = []
    for row_tap in range(3):
        weight_cols = []
        for col_tap in range(3):
            window = padded[:, :, row_tap : row_tap + extent, col_tap : col_tap + extent]
            weight_cols.append(
                jnp.einsum("noxy,ncxy->oc", grad_full, window, preferred_element_type=jnp.float32)
            )
            spread = jnp.einsum(
                "oc,noxy->ncxy",
                weight[:, :, row_tap, col_tap],
                grad_full,
                preferred_element_type=jnp.float32,
            )
            grad_padded = grad_padded.at[
                :, :, row_tap : row_tap + extent, col_tap : col_tap + extent
            ].add(spread)
        weight_rows.append(jnp.stack(weight_cols, axis=-1))
    return (jnp.stack(weight_rows, axis=2), grad_padded)


def add_returned(grad_padded, returned):
    interior = grad_padded[:, :, 1:-1, 1:-1]
    interior = interior.at[:, :, 0, :].add(returned[:, 0])
    interior = interior.at[:, :, -1, :].add(returned[:, 1])
    interior = interior.at[:, :, :, 0].add(returned[:, 2])
    interior = interior.at[:, :, :, -1].add(returned[:, 3])
    return interior.astype(jnp.bfloat16)


def flatten_pixels(field):
    return field.reshape(field.shape[0], field.shape[1], -1)


def on_device(inputs, gluing, conv_weight, level_weight, cotangent):
    inputs = inputs.reshape(inputs.shape[0], inputs.shape[1], S, S)
    cotangent = cotangent.reshape(cotangent.shape[0], cotangent.shape[1], S // 2, S // 2)
    chan_width = inputs.shape[1]
    chan_first = lax.axis_index("chan") * chan_width
    picker = make_picker(gluing)
    conv_in = lax.dynamic_slice_in_dim(conv_weight, chan_first, chan_width, 1)
    level_in = lax.dynamic_slice_in_dim(level_weight, chan_first, chan_width, 1)
    strips = edge_strips(inputs)
    halo_cells = picker(
        jnp.zeros_like(strips), lax.all_gather(strips, "tile", axis=0, tiled=True), jnp.int32(0)
    )
    padded_own = assemble(inputs, orient(halo_cells, gluing))
    partial_pre = conv_three(padded_own, conv_in)
    pre_act = lax.psum_scatter(partial_pre, "chan", scatter_dimension=1, tiled=True)
    hidden = jax.nn.gelu(pre_act).astype(jnp.bfloat16)
    level_part = conv_two(hidden, level_in)
    level = lax.psum_scatter(level_part, "chan", scatter_dimension=1, tiled=True).astype(
        jnp.bfloat16
    )
    cot_full = lax.all_gather(cotangent, "chan", axis=1, tiled=True)
    grad_level, grad_hidden = level_grads(hidden, cot_full, level_in)
    unused, pullback = jax.vjp(jax.nn.gelu, pre_act)
    grad_pre = pullback(grad_hidden)[0].astype(jnp.bfloat16)
    grad_full = lax.all_gather(grad_pre, "chan", axis=1, tiled=True)
    grad_conv, grad_padded = conv_grads(padded_own, grad_full, conv_in)
    grad_conv, grad_level = lax.psum((grad_conv, grad_level), "tile")
    rims = border_strips(grad_padded).astype(jnp.bfloat16)
    returned = picker(
        jnp.zeros_like(rims), lax.all_gather(rims, "tile", axis=0, tiled=True), jnp.int32(0)
    )
    returned = orient(returned, gluing).astype(jnp.float32)
    grad_inputs = add_returned(grad_padded, returned)
    return (flatten_pixels(level), flatten_pixels(grad_inputs), grad_conv, grad_level)


def solution(mesh):
    return jax.shard_map(
        on_device,
        mesh=mesh,
        in_specs=(
            P("tile", "chan", None),
            P("tile", None, None),
            P(),
            P(),
            P("tile", "chan", None),
        ),
        out_specs=(
            P("tile", "chan", None),
            P("tile", "chan", None),
            P(None, "chan", None, None),
            P(None, "chan", None, None),
        ),
        check_vma=False,
    )
```

profile of v0, /device:TPU:1, one launch (start us, length us, event | category | flops | bytes accessed | tf_op | source)
XLA Modules:
  0.0 1141.6 jit_solution(13108972950838934719)
XLA Ops:
  16.2 104.5 %all-gather.4.cloned.1.call-done = bf16[128,4,32,64]{3,2,0,1:T(8,128)(2,1)} async-done(((bf16[2,4,32,64]{3,2,0,1:T(8,128)(2,1)}), bf16[128,4,32,64]{3,2,0,1:T(8,128)(2,1)}) %all-gather.4.cloned.1.call-update) | async-done | bytes 2097168 | tf_op jit(solution)/shard_map/all_gather | solution.py:161
  120.7 5.6 copy.407
  134.6 4.2 maximum_maximum_fusion
  150.2 15.4 %fusion.25 = f32[2,64,64,64]{3,2,1,0:T(8,128)} fusion(bf16[2,32,64,1]{3,1,2,0:T(8,128)(2,1)S(1)} %copy-done.12, bf16[2,32,64,64]{3,1,2,0:T(8,128)(2,1)S(1)} %copy.410, bf16[64,64,3,3]{1,0,3,2:T(8,128)(2,1)S(1)} %copy-done, s32[]{:T(128)S(6)} %select_n.26, s32[]{:T(128)S(6)} %add.205, s32[]{:T(128)S(6)} %add.206), kind=kOutput, calls=%fused_computation.75 | convolution fusion | flops 34603008 | bytes 4210700 | tf_op jit(solution)/shard_map/oc,ncxy->noxy/dot_general | solution.py:60
  168.9 10.7 bitcast_add_fusion
  179.6 5.7 copy.420
  189.8 47.9 %all_gather.13 = bf16[2,128,32,32]{3,2,0,1:T(8,128)(2,1)} all-gather(bf16[2,64,32,32]{3,2,0,1:T(8,128)(2,1)S(1)} %copy.432), channel_id=1, replica_groups=mesh['tile'=64,'chan'=2] {'chan'}, dimensions={1}, use_global_device_ids=true | all-gather | bytes 786432 | tf_op jit(solution)/shard_map/all_gather | solution.py:171
  247.6 6.4 maximum_bitcast_fusion
  253.9 4.3 pad_maximum_fusion
  264.1 5.7 fusion.6
  269.7 32.0 %slice.621 = bf16[2,32,32,32]{3,1,2,0:T(8,128)(2,1)} slice(bf16[2,32,64,64]{3,1,2,0:T(8,128)(2,1)} %get-tuple-element.198), slice={[0:2:1], [0:32:1], [0:64:2], [1:64:2]} | slice | bytes 262144 | tf_op jit(solution)/shard_map/slice | solution.py:75
  301.7 32.0 %slice.619 = bf16[2,32,32,32]{3,1,2,0:T(8,128)(2,1)} slice(bf16[2,32,64,64]{3,1,2,0:T(8,128)(2,1)} %get-tuple-element.198), slice={[0:2:1], [0:32:1], [0:64:2], [0:64:2]} | slice | bytes 262144 | tf_op jit(solution)/shard_map/slice | solution.py:75
  333.8 27.9 %slice.625 = bf16[2,32,32,32]{3,1,2,0:T(8,128)(2,1)S(1)} slice(bf16[2,32,64,64]{3,1,2,0:T(8,128)(2,1)} %get-tuple-element.198), slice={[0:2:1], [0:32:1], [1:64:2], [1:64:2]} | slice | bytes 262144 | tf_op jit(solution)/shard_map/slice | solution.py:75
  361.7 32.0 %slice.623 = bf16[2,32,32,32]{3,1,2,0:T(8,128)(2,1)} slice(bf16[2,32,64,64]{3,1,2,0:T(8,128)(2,1)} %get-tuple-element.198), slice={[0:2:1], [0:32:1], [1:64:2], [0:64:2]} | slice | bytes 262144 | tf_op jit(solution)/shard_map/slice | solution.py:75
  414.9 21.4 %all-gather.6.cloned.1.call-done = bf16[2,64,64,64]{3,2,0,1:T(8,128)(2,1)} async-done(((bf16[2,32,64,64]{3,2,0,1:T(8,128)(2,1)}), bf16[2,64,64,64]{3,2,0,1:T(8,128)(2,1)}) %all-gather.6.cloned.1.call-update) | async-done | bytes 1048592 | tf_op jit(solution)/shard_map/all_gather | solution.py:175
  457.8 4.5 copy.510
  462.3 4.4 reshape.665
  477.8 11.3 scatter-add.45
  489.1 5.5 add_select_fusion
  494.6 11.3 scatter-add.46
  509.6 23.8 %scatter-add.49 = f32[2,32,66,66]{2,1,0,3:T(8,128)S(1)} dynamic-update-slice(f32[2,32,66,66]{2,1,0,3:T(8,128)S(1)} %scatter-add.46, f32[2,32,64,64]{2,1,0,3:T(8,128)} %slice_add_fusion.7, s32[]{:T(128)} %constant.397.clone.1, s32[]{:T(128)} %constant.397.clone.1, s32[]{:T(128)} %constant.395.clone.1, s32[]{:T(128)} %constant.397.clone.1) | dynamic-update-slice | bytes 2097156 | tf_op jit(solution)/shard_map/scatter-add | solution.py:133
  537.0 23.8 %scatter-add.50 = f32[2,32,66,66]{2,1,0,3:T(8,128)S(1)} dynamic-update-slice(f32[2,32,66,66]{2,1,0,3:T(8,128)S(1)} %scatter-add.49, f32[2,32,64,64]{2,1,0,3:T(8,128)} %slice_add_fusion.6, s32[]{:T(128)} %constant.397.clone.1, s32[]{:T(128)} %constant.397.clone.1, s32[]{:T(128)} %constant.395.clone.1, s32[]{:T(128)} %constant.395.clone.1) | dynamic-update-slice | bytes 2097156 | tf_op jit(solution)/shard_map/scatter-add | solution.py:133
  564.4 23.8 %scatter-add.51 = f32[2,32,66,66]{2,1,0,3:T(8,128)S(1)} dynamic-update-slice(f32[2,32,66,66]{2,1,0,3:T(8,128)S(1)} %scatter-add.50, f32[2,32,64,64]{2,1,0,3:T(8,128)} %slice_add_fusion.5, s32[]{:T(128)} %constant.397.clone.1, s32[]{:T(128)} %constant.397.clone.1, s32[]{:T(128)} %constant.395.clone.1, s32[]{:T(128)} %constant.411.clone.1) | dynamic-update-slice | bytes 2097156 | tf_op jit(solution)/shard_map/scatter-add | solution.py:133
  591.8 23.8 %scatter-add.54 = f32[2,32,66,66]{2,1,0,3:T(8,128)S(1)} dynamic-update-slice(f32[2,32,66,66]{2,1,0,3:T(8,128)S(1)} %scatter-add.51, f32[2,32,64,64]{2,1,0,3:T(8,128)} %slice_add_fusion.4, s32[]{:T(128)} %constant.397.clone.1, s32[]{:T(128)} %constant.397.clone.1, s32[]{:T(128)} %constant.411.clone.1, s32[]{:T(128)} %constant.397.clone.1) | dynamic-update-slice | bytes 2097156 | tf_op jit(solution)/shard_map/scatter-add | solution.py:133
  619.2 23.8 %scatter-add.55 = f32[2,32,66,66]{2,1,0,3:T(8,128)S(1)} dynamic-update-slice(f32[2,32,66,66]{2,1,0,3:T(8,128)S(1)} %scatter-add.54, f32[2,32,64,64]{2,1,0,3:T(8,128)} %slice_add_fusion.3, s32[]{:T(128)} %constant.397.clone.1, s32[]{:T(128)} %constant.397.clone.1, s32[]{:T(128)} %constant.411.clone.1, s32[]{:T(128)} %constant.395.clone.1) | dynamic-update-slice | bytes 2097156 | tf_op jit(solution)/shard_map/scatter-add | solution.py:133
  646.6 23.9 %scatter-add.56 = f32[2,32,66,66]{2,1,0,3:T(8,128)S(1)} dynamic-update-slice(f32[2,32,66,66]{2,1,0,3:T(8,128)S(1)} %scatter-add.55, f32[2,32,64,64]{2,1,0,3:T(8,128)} %slice_add_fusion.2, s32[]{:T(128)} %constant.397.clone.1, s32[]{:T(128)} %constant.397.clone.1, s32[]{:T(128)} %constant.411.clone.1, s32[]{:T(128)} %constant.411.clone.1) | dynamic-update-slice | bytes 2097156 | tf_op jit(solution)/shard_map/scatter-add | solution.py:133
  679.3 278.6 %all-reduce.4.cloned.1.call-done = (f32[64,32,3,3]{0,1,3,2:T(8,128)}, f32[128,32,2,2]{0,1,3,2:T(8,128)}) async-done(((f32[64,32,3,3]{0,1,3,2:T(8,128)}, f32[128,32,2,2]{0,1,3,2:T(8,128)}), (f32[64,32,3,3]{0,1,3,2:T(8,128)}, f32[128,32,2,2]{0,1,3,2:T(8,128)})) %all-reduce.4.cloned.1.call-update) | async-done | bytes 139280 | tf_op jit(solution)/shard_map/psum | solution.py:177
  959.4 24.5 %reduce-scatter.7.cloned.1.call-done = f32[64,2048]{1,0:T(8,128)} async-done(((f32[128,2048]{1,0:T(8,128)}), f32[64,2048]{1,0:T(8,128)}) %reduce-scatter.7.cloned.1.call-update) | async-done | bytes 524304
  989.7 101.2 %all-gather.8.cloned.1.call-done = bf16[128,4,32,64]{3,2,0,1:T(8,128)(2,1)} async-done(((bf16[2,4,32,64]{3,2,0,1:T(8,128)(2,1)}), bf16[128,4,32,64]{3,2,0,1:T(8,128)(2,1)}) %all-gather.8.cloned.1.call-update) | async-done | bytes 2097168 | tf_op jit(solution)/shard_map/all_gather | solution.py:180
  1090.9 5.5 copy.458
  1109.2 5.2 scatter-add.59
  1118.0 12.7 %scatter-add.60 = f32[2,32,64,64]{2,1,0,3:T(8,128)S(1)} dynamic-update-slice(f32[2,32,64,64]{2,1,0,3:T(8,128)S(1)} %scatter-add.59, f32[2,32,1,64]{2,1,0,3:T(8,128)} %slice_add_fusion, s32[]{:T(128)} %constant.397.clone.1, s32[]{:T(128)} %constant.397.clone.1, s32[]{:T(128)} %constant.414.clone.1, s32[]{:T(128)} %constant.397.clone.1) | dynamic-update-slice | bytes 32772 | tf_op jit(solution)/shard_map/scatter-add | solution.py:141
  (201 shorter events, 163.6 us)
Async XLA Ops:
  7.2 6.0 copy-start
  7.2 113.5 %all-gather.4.cloned.1.call-start = ((), (), s32[]{:S(2)}) async-start(), calls=%async_computation.2 | async-start | bytes 4259840 | tf_op jit(solution)/shard_map/all_gather | solution.py:161
  9.4 3.3 copy-start.28
  11.6 252.5 %reduce-scatter.5.cloned.1.call-start = ((), (), s32[]{:S(2)}) async-start(), calls=%async_computation.3 | async-start | bytes 6291456 | tf_op jit(solution)/shard_map/reduce_scatter | solution.py:165
  12.9 116.4 %copy-start.29 = (pred[2,4]{0,1:T(4,128)(4,1)}, pred[2,4]{0,1:T(4,128)(4,1)S(1)}, u32[]{:S(2)}) copy-start(pred[2,4]{0,1:T(4,128)(4,1)S(1)} %copy.406) | copy-start | bytes 28
  13.0 116.3 %copy-start.31 = (pred[2,4]{0,1:T(4,128)(4,1)}, pred[2,4]{0,1:T(4,128)(4,1)S(1)}, u32[]{:S(2)}) copy-start(pred[2,4]{0,1:T(4,128)(4,1)S(1)} %copy.405) | copy-start | bytes 28
  13.1 116.2 %copy-start.33 = (pred[2,4]{0,1:T(4,128)(4,1)}, pred[2,4]{0,1:T(4,128)(4,1)S(1)}, u32[]{:S(2)}) copy-start(pred[2,4]{0,1:T(4,128)(4,1)S(1)} %copy.404) | copy-start | bytes 28
  13.1 113.2 %copy-start.27 = (s32[1024]{0:T(1024)}, s32[1024]{0:T(1024)S(1)}, u32[]{:S(2)}) copy-start(s32[1024]{0:T(1024)S(1)} %pad_clamp_fusion) | copy-start | bytes 12292
  138.8 30.1 %copy-start.7 = (bf16[2,32,65,66]{3,1,2,0:T(8,128)(2,1)}, bf16[2,32,65,66]{3,1,2,0:T(8,128)(2,1)S(1)}, u32[]{:S(2)}) copy-start(bf16[2,32,65,66]{3,1,2,0:T(8,128)(2,1)S(1)} %get-tuple-element.196) | copy-start | bytes 1647364
  146.9 3.3 copy-start.12
  150.2 15.4 %copy-start.10 = (bf16[2,32,64,1]{3,1,2,0:T(8,128)(2,1)S(1)}, bf16[2,32,64,1]{3,1,2,0:T(8,128)(2,1)}, u32[]{:S(2)}) copy-start(bf16[2,32,64,1]{3,1,2,0:T(8,128)(2,1)} %copy.409) | copy-start | bytes 24580
  165.6 3.3 copy-start.4
  185.3 251.1 %all-gather.6.cloned.1.call-start = ((), (), s32[]{:S(2)}) async-start(), calls=%async_computation.4 | async-start | bytes 3145728 | tf_op jit(solution)/shard_map/all_gather | solution.py:175
  237.7 3.3 copy-start.26
  258.2 5.2 copy-start.35
  393.6 3.7 copy-start.15
  393.6 4.2 copy-start.18
  397.8 4.0 copy-start.14
  399.3 558.6 %all-reduce.4.cloned.1.call-start = ((), (), s32[]{:S(2)}) async-start(), calls=%async_computation.7 | async-start | bytes 425984 | tf_op jit(solution)/shard_map/psum | solution.py:177
  399.7 3.1 copy-start.16
  404.9 5.8 copy-start.20
  406.1 5.9 copy-start.23
  412.3 24.1 %copy-start.6 = (bf16[2,32,65,66]{3,1,2,0:T(8,128)(2,1)S(1)}, bf16[2,32,65,66]{3,1,2,0:T(8,128)(2,1)}, u32[]{:S(2)}) copy-start(bf16[2,32,65,66]{3,1,2,0:T(8,128)(2,1)} %copy-done.5) | copy-start | bytes 1647364
  436.3 3.8 copy-start.21
  454.5 2.9 copy-start.17
  457.4 526.6 %reduce-scatter.7.cloned.1.call-start = ((), (), s32[]{:S(2)}) async-start(), calls=%async_computation.6 | async-start | bytes 1572864
  466.7 624.2 %all-gather.8.cloned.1.call-start = ((), (), s32[]{:S(2)}) async-start(), calls=%async_computation.5 | async-start | bytes 4259840 | tf_op jit(solution)/shard_map/all_gather | solution.py:180
  989.7 109.6 %copy-start.30 = (pred[2,4]{0,1:T(4,128)(4,1)S(1)}, pred[2,4]{0,1:T(4,128)(4,1)}, u32[]{:S(2)}) copy-start(pred[2,4]{0,1:T(4,128)(4,1)} %copy-done.29) | copy-start | bytes 28
  989.7 109.6 %copy-start.32 = (pred[2,4]{0,1:T(4,128)(4,1)S(1)}, pred[2,4]{0,1:T(4,128)(4,1)}, u32[]{:S(2)}) copy-start(pred[2,4]{0,1:T(4,128)(4,1)} %copy-done.31) | copy-start | bytes 28
  989.7 109.8 %copy-start.34 = (pred[2,4]{0,1:T(4,128)(4,1)S(1)}, pred[2,4]{0,1:T(4,128)(4,1)}, u32[]{:S(2)}) copy-start(pred[2,4]{0,1:T(4,128)(4,1)} %copy-done.33) | copy-start | bytes 28
  1106.3 2.9 copy-start.3
  1131.0 2.9 copy-start.25
  (10 other events, 17.7 us)
Sparse Core Ops, SparseCore 0:
  11.7 109.0 all-gather.3
  185.4 78.0 reduce-scatter.4
  399.4 36.9 all-gather.5
  457.5 500.3 all-reduce.3
  960.1 23.8 reduce-scatter.6
  985.5 105.3 all-gather.7
where the time goes:
time: 1160 us; the launch traced here: 1140 us
  waiting for transfers between devices  530 us (46%)
  local copies, waits for them, and re-layouts  411 us (35%)
  matrix products  104 us (9%)
  blocking collectives  47.9 us (4%)
  other arithmetic  32.2 us (3%)
  between operations  15 us (1%)
    psum x1, waiting for transfers between devices, on_device(): grad_conv, grad_level = lax.psum((grad_conv, grad_level), 'tile')  279 us
    scatter-add x9, local copies, waits for them, and re-layouts, conv_grads(): grad_padded = grad_padded.at[:, :, row_tap:row_tap + extent, col_tap:col_...  166 us
    slice x8, local copies, waits for them, and re-layouts, conv_two(): hidden[:, :, row_tap::2, col_tap::2].reshape(tile_count, chan_count, -1)  129 us
    all_gather x1, waiting for transfers between devices, on_device(): lax.all_gather(strips, 'tile', axis=0, tiled=True)  105 us
    all_gather x1, waiting for transfers between devices, on_device(): lax.all_gather(rims, 'tile', axis=0, tiled=True)  101 us
    all_gather x1, blocking collectives, on_device(): cot_full = lax.all_gather(cotangent, 'chan', axis=1, tiled=True)  47.9 us
    dot_general x9, matrix products, conv_three(): jnp.einsum('oc,ncxy->noxy', weight[:, :, row_tap, col_tap], padded[:, :,...  43.8 us
    dot_general x9, matrix products, conv_grads(): jnp.einsum('oc,noxy->ncxy', weight[:, :, row_tap, col_tap], grad_full, pr...  31.3 us
  transfers between devices with their start and end apart: 6, of which 5 were waited for; matrix products, arithmetic and copies ran while one was open for 24% of the time, Pallas kernels for 0%

commit v1 on v0

--- a/solution.py
+++ b/solution.py
@@ -158,7 +158,11 @@
     level_in = lax.dynamic_slice_in_dim(level_weight, chan_first, chan_width, 1)
     strips = edge_strips(inputs)
     halo_cells = picker(
-        jnp.zeros_like(strips), lax.all_gather(strips, "tile", axis=0, tiled=True), jnp.int32(0)
+        jnp.zeros_like(strips),
+        jnp.concatenate(
+            lax.all_to_all(jnp.stack([strips] * lax.axis_size("tile")), "tile", 0, 0), axis=0
+        ),
+        jnp.int32(0),
     )
     padded_own = assemble(inputs, orient(halo_cells, gluing))
     partial_pre = conv_three(padded_own, conv_in)

time: 1160 us -> 1100 us (0.948)
  waiting for transfers between devices: 530 us -> 447 us
    all_gather x1 -> x0, waiting for transfers between devices: 105 us -> none  [on_device(): lax.all_gather(strips, 'tile', axis=0, tiled=True)]
    all_to_all x0 -> x1, waiting for transfers between devices: none -> 24.6 us  [on_device(): lax.all_to_all(jnp.stack([strips] * lax.axis_size('tile')), 'tile', 0, 0)]
    unnamed x83 -> x95, local copies, waits for them, and re-layouts: 25.2 us -> 41.3 us
    unnamed x7 -> x6, waiting for transfers between devices: 24.6 us -> 24.6 us
  transfers between devices with their start and end apart: 6 -> 6, of which waited for: 5 -> 5; matrix products, arithmetic and copies ran while one was open for 24% -> 25% of each run, Pallas kernels for 0% -> 0%
where the time goes in v1:
time: 1100 us; the launch traced here: 1080 us
  waiting for transfers between devices  447 us (41%)
  local copies, waits for them, and re-layouts  422 us (38%)
  matrix products  94.2 us (9%)
  blocking collectives  58.6 us (5%)
  other arithmetic  33.8 us (3%)
  between operations  14.7 us (1%)
  starting transfers between devices  12 us (1%)
    psum x1, waiting for transfers between devices, on_device(): grad_conv, grad_level = lax.psum((grad_conv, grad_level), 'tile')  279 us
    scatter-add x9, local copies, waits for them, and re-layouts, conv_grads(): grad_padded = grad_padded.at[:, :, row_tap:row_tap + extent, col_tap:col_...  165 us
    slice x8, local copies, waits for them, and re-layouts, conv_two(): hidden[:, :, row_tap::2, col_tap::2].reshape(tile_count, chan_count, -1)  129 us
    all_gather x1, waiting for transfers between devices, on_device(): lax.all_gather(rims, 'tile', axis=0, tiled=True)  101 us
    all_gather x1, blocking collectives, on_device(): cot_full = lax.all_gather(cotangent, 'chan', axis=1, tiled=True)  58.6 us
    unnamed x95, local copies, waits for them, and re-layouts  41.3 us
    dot_general x9, matrix products, conv_three(): jnp.einsum('oc,ncxy->noxy', weight[:, :, row_tap, col_tap], padded[:, :,...  33.3 us
    dot_general x9, matrix products, conv_grads(): jnp.einsum('oc,noxy->ncxy', weight[:, :, row_tap, col_tap], grad_full, pr...  31.1 us
  transfers between devices with their start and end apart: 6, of which 5 were waited for; matrix products, arithmetic and copies ran while one was open for 25% of the time, Pallas kernels for 0%

profile of v1, /device:TPU:1, one launch (start us, length us, event | category | flops | bytes accessed | tf_op | source)
XLA Modules:
  0.0 1082.4 jit_solution(14326801976286795537)
XLA Ops:
  13.9 7.9 reshape.667
  21.8 11.0 %all-to-all-start = ((bf16[64,2,8192]{2,1,0:T(2,128)(2,1)}), bf16[64,2,8192]{2,1,0:T(2,128)(2,1)}, u32[]{:S(2)}, u32[]{:S(2)}) async-start(bf16[64,2,8192]{2,1,0:T(2,128)(2,1)} %reshape.667), calls=%async_computation | async-start | bytes 4194304 | tf_op jit(solution)/shard_map/all_to_all | solution.py:163
  37.1 24.6 %all-to-all-done = bf16[64,2,8192]{2,1,0:T(2,128)(2,1)} async-done(((bf16[64,2,8192]{2,1,0:T(2,128)(2,1)}), bf16[64,2,8192]{2,1,0:T(2,128)(2,1)}, u32[]{:S(2)}, u32[]{:S(2)}) %all-to-all-start) | async-done | bytes 2097184 | tf_op jit(solution)/shard_map/all_to_all | solution.py:163
  61.7 8.4 reshape.668
  100.7 12.2 %bitcast_add_fusion = f32[2,64,64,64]{1,3,2,0:T(8,128)} fusion(f32[2,64,64,64]{3,2,1,0:T(8,128)} %fusion.10, f32[2,64,64,64]{3,2,1,0:T(8,128)} %fusion.13, f32[2,64,64,64]{3,2,1,0:T(8,128)} %fusion.25, f32[64,2,64,64]{0,3,2,1:T(8,128)S(1)} %copy-done.4, f32[2,64,64,64]{3,2,1,0:T(8,128)} %fusion.24, f32[2,64,64,64]{3,2,1,0:T(8,128)} %fusion.16, ...), kind=kOutput, calls=%fused_computation.3 | convolution fusion | flops 37748736 | bytes 36716552 | tf_op jit(solution)/shard_map/oc,ncxy->noxy/dot_general | solution.py:60
  112.9 5.7 copy.571
  122.2 58.6 %all_gather.9 = bf16[2,128,32,32]{3,2,0,1:T(8,128)(2,1)} all-gather(bf16[2,64,32,32]{3,2,0,1:T(8,128)(2,1)} %copy.583), channel_id=1, replica_groups=mesh['tile'=64,'chan'=2] {'chan'}, dimensions={1}, use_global_device_ids=true | all-gather | bytes 786432 | tf_op jit(solution)/shard_map/all_gather | solution.py:175
  191.3 6.4 maximum_bitcast_fusion
  197.7 4.2 pad_maximum_fusion
  207.8 5.7 fusion.6
  213.5 32.0 %slice.621 = bf16[2,32,32,32]{3,1,2,0:T(8,128)(2,1)} slice(bf16[2,32,64,64]{3,1,2,0:T(8,128)(2,1)} %get-tuple-element.206), slice={[0:2:1], [0:32:1], [0:64:2], [1:64:2]} | slice | bytes 262144 | tf_op jit(solution)/shard_map/slice | solution.py:75
  245.5 32.0 %slice.619 = bf16[2,32,32,32]{3,1,2,0:T(8,128)(2,1)} slice(bf16[2,32,64,64]{3,1,2,0:T(8,128)(2,1)} %get-tuple-element.206), slice={[0:2:1], [0:32:1], [0:64:2], [0:64:2]} | slice | bytes 262144 | tf_op jit(solution)/shard_map/slice | solution.py:75
  277.5 27.9 %slice.625 = bf16[2,32,32,32]{3,1,2,0:T(8,128)(2,1)S(1)} slice(bf16[2,32,64,64]{3,1,2,0:T(8,128)(2,1)} %get-tuple-element.206), slice={[0:2:1], [0:32:1], [1:64:2], [1:64:2]} | slice | bytes 262144 | tf_op jit(solution)/shard_map/slice | solution.py:75
  305.4 31.9 %slice.623 = bf16[2,32,32,32]{3,1,2,0:T(8,128)(2,1)} slice(bf16[2,32,64,64]{3,1,2,0:T(8,128)(2,1)} %get-tuple-element.206), slice={[0:2:1], [0:32:1], [1:64:2], [0:64:2]} | slice | bytes 262144 | tf_op jit(solution)/shard_map/slice | solution.py:75
  359.7 17.8 %all-gather.3.cloned.1.call-done = bf16[2,64,64,64]{3,2,0,1:T(8,128)(2,1)} async-done(((bf16[2,32,64,64]{3,2,0,1:T(8,128)(2,1)}), bf16[2,64,64,64]{3,2,0,1:T(8,128)(2,1)}) %all-gather.3.cloned.1.call-update) | async-done | bytes 1048592 | tf_op jit(solution)/shard_map/all_gather | solution.py:179
  399.2 4.5 copy.661
  403.6 4.4 reshape.663
  419.1 11.2 %scatter-add.45 = f32[2,32,66,66]{2,1,0,3:T(8,128)S(1)} dynamic-update-slice(f32[2,32,66,66]{2,1,0,3:T(8,128)S(1)} %scatter-add.44, f32[2,32,64,64]{2,1,0,3:T(8,128)} %bitcast_add_fusion.5, s32[]{:T(128)} %constant.397.clone.1, s32[]{:T(128)} %constant.397.clone.1, s32[]{:T(128)} %bitcast.75, s32[]{:T(128)} %bitcast.76) | dynamic-update-slice | bytes 2097156 | tf_op jit(solution)/shard_map/scatter-add | solution.py:133
  430.2 5.4 add_select_fusion
  435.7 11.2 %scatter-add.46 = f32[2,32,66,66]{2,1,0,3:T(8,128)S(1)} dynamic-update-slice(f32[2,32,66,66]{2,1,0,3:T(8,128)S(1)} %scatter-add.45, f32[2,32,64,64]{2,1,0,3:T(8,128)} %add_select_fusion, s32[]{:T(128)} %constant.397.clone.1, s32[]{:T(128)} %constant.397.clone.1, s32[]{:T(128)} %bitcast.79, s32[]{:T(128)} %bitcast.80) | dynamic-update-slice | bytes 2097156 | tf_op jit(solution)/shard_map/scatter-add | solution.py:133
  450.5 23.8 %scatter-add.49 = f32[2,32,66,66]{2,1,0,3:T(8,128)S(1)} dynamic-update-slice(f32[2,32,66,66]{2,1,0,3:T(8,128)S(1)} %scatter-add.46, f32[2,32,64,64]{2,1,0,3:T(8,128)} %slice_add_fusion.7, s32[]{:T(128)} %constant.397.clone.1, s32[]{:T(128)} %constant.397.clone.1, s32[]{:T(128)} %constant.395.clone.1, s32[]{:T(128)} %constant.397.clone.1) | dynamic-update-slice | bytes 2097156 | tf_op jit(solution)/shard_map/scatter-add | solution.py:133
  477.9 23.8 %scatter-add.50 = f32[2,32,66,66]{2,1,0,3:T(8,128)S(1)} dynamic-update-slice(f32[2,32,66,66]{2,1,0,3:T(8,128)S(1)} %scatter-add.49, f32[2,32,64,64]{2,1,0,3:T(8,128)} %slice_add_fusion.6, s32[]{:T(128)} %constant.397.clone.1, s32[]{:T(128)} %constant.397.clone.1, s32[]{:T(128)} %constant.395.clone.1, s32[]{:T(128)} %constant.395.clone.1) | dynamic-update-slice | bytes 2097156 | tf_op jit(solution)/shard_map/scatter-add | solution.py:133
  505.3 23.8 %scatter-add.51 = f32[2,32,66,66]{2,1,0,3:T(8,128)S(1)} dynamic-update-slice(f32[2,32,66,66]{2,1,0,3:T(8,128)S(1)} %scatter-add.50, f32[2,32,64,64]{2,1,0,3:T(8,128)} %slice_add_fusion.5, s32[]{:T(128)} %constant.397.clone.1, s32[]{:T(128)} %constant.397.clone.1, s32[]{:T(128)} %constant.395.clone.1, s32[]{:T(128)} %constant.411.clone.1) | dynamic-update-slice | bytes 2097156 | tf_op jit(solution)/shard_map/scatter-add | solution.py:133
  532.7 23.8 %scatter-add.54 = f32[2,32,66,66]{2,1,0,3:T(8,128)S(1)} dynamic-update-slice(f32[2,32,66,66]{2,1,0,3:T(8,128)S(1)} %scatter-add.51, f32[2,32,64,64]{2,1,0,3:T(8,128)} %slice_add_fusion.4, s32[]{:T(128)} %constant.397.clone.1, s32[]{:T(128)} %constant.397.clone.1, s32[]{:T(128)} %constant.411.clone.1, s32[]{:T(128)} %constant.397.clone.1) | dynamic-update-slice | bytes 2097156 | tf_op jit(solution)/shard_map/scatter-add | solution.py:133
  560.1 23.8 %scatter-add.55 = f32[2,32,66,66]{2,1,0,3:T(8,128)S(1)} dynamic-update-slice(f32[2,32,66,66]{2,1,0,3:T(8,128)S(1)} %scatter-add.54, f32[2,32,64,64]{2,1,0,3:T(8,128)} %slice_add_fusion.3, s32[]{:T(128)} %constant.397.clone.1, s32[]{:T(128)} %constant.397.clone.1, s32[]{:T(128)} %constant.411.clone.1, s32[]{:T(128)} %constant.395.clone.1) | dynamic-update-slice | bytes 2097156 | tf_op jit(solution)/shard_map/scatter-add | solution.py:133
  587.5 23.9 %scatter-add.56 = f32[2,32,66,66]{2,1,0,3:T(8,128)S(1)} dynamic-update-slice(f32[2,32,66,66]{2,1,0,3:T(8,128)S(1)} %scatter-add.55, f32[2,32,64,64]{2,1,0,3:T(8,128)} %slice_add_fusion.2, s32[]{:T(128)} %constant.397.clone.1, s32[]{:T(128)} %constant.397.clone.1, s32[]{:T(128)} %constant.411.clone.1, s32[]{:T(128)} %constant.411.clone.1) | dynamic-update-slice | bytes 2097156 | tf_op jit(solution)/shard_map/scatter-add | solution.py:133
  620.3 278.8 %all-reduce.4.cloned.1.call-done = (f32[64,32,3,3]{0,1,3,2:T(8,128)}, f32[128,32,2,2]{0,1,3,2:T(8,128)}) async-done(((f32[64,32,3,3]{0,1,3,2:T(8,128)}, f32[128,32,2,2]{0,1,3,2:T(8,128)}), (f32[64,32,3,3]{0,1,3,2:T(8,128)}, f32[128,32,2,2]{0,1,3,2:T(8,128)})) %all-reduce.4.cloned.1.call-update) | async-done | bytes 139280 | tf_op jit(solution)/shard_map/psum | solution.py:181
  900.6 24.5 %reduce-scatter.7.cloned.1.call-done = f32[64,2048]{1,0:T(8,128)} async-done(((f32[128,2048]{1,0:T(8,128)}), f32[64,2048]{1,0:T(8,128)}) %reduce-scatter.7.cloned.1.call-update) | async-done | bytes 524304
  930.9 101.2 %all-gather.5.cloned.1.call-done = bf16[128,4,32,64]{3,2,0,1:T(8,128)(2,1)} async-done(((bf16[2,4,32,64]{3,2,0,1:T(8,128)(2,1)}), bf16[128,4,32,64]{3,2,0,1:T(8,128)(2,1)}) %all-gather.5.cloned.1.call-update) | async-done | bytes 2097168 | tf_op jit(solution)/shard_map/all_gather | solution.py:184
  1032.1 5.5 copy.609
  1050.3 5.2 scatter-add.59
  1059.2 12.7 %scatter-add.60 = f32[2,32,64,64]{2,1,0,3:T(8,128)S(1)} dynamic-update-slice(f32[2,32,64,64]{2,1,0,3:T(8,128)S(1)} %scatter-add.59, f32[2,32,1,64]{2,1,0,3:T(8,128)} %slice_add_fusion, s32[]{:T(128)} %constant.397.clone.1, s32[]{:T(128)} %constant.397.clone.1, s32[]{:T(128)} %constant.414.clone.1, s32[]{:T(128)} %constant.397.clone.1) | dynamic-update-slice | bytes 32772 | tf_op jit(solution)/shard_map/scatter-add | solution.py:141
  (213 shorter events, 173.9 us)
Async XLA Ops:
  7.2 26.8 %copy-start = (bf16[64,64,3,3]{1,0,3,2:T(8,128)(2,1)S(1)}, bf16[64,64,3,3]{1,0,3,2:T(8,128)(2,1)}, u32[]{:S(2)}) copy-start(bf16[64,64,3,3]{1,0,3,2:T(8,128)(2,1)} %param.35) | copy-start | bytes 221188
  21.8 39.9 %all-to-all-start = ((bf16[64,2,8192]{2,1,0:T(2,128)(2,1)}), bf16[64,2,8192]{2,1,0:T(2,128)(2,1)}, u32[]{:S(2)}, u32[]{:S(2)}) async-start(bf16[64,2,8192]{2,1,0:T(2,128)(2,1)} %reshape.667), calls=%async_computation | async-start | bytes 4194304 | tf_op jit(solution)/shard_map/all_to_all | solution.py:163
  32.8 175.0 %reduce-scatter.5.cloned.1.call-start = ((), (), s32[]{:S(2)}) async-start(), calls=%async_computation.3 | async-start | bytes 6291456 | tf_op jit(solution)/shard_map/reduce_scatter | solution.py:169
  33.8 39.3 %copy-start.34 = (pred[2,4]{0,1:T(4,128)(4,1)}, pred[2,4]{0,1:T(4,128)(4,1)S(1)}, u32[]{:S(2)}) copy-start(pred[2,4]{0,1:T(4,128)(4,1)S(1)} %copy.557) | copy-start | bytes 28
  33.9 39.2 %copy-start.36 = (pred[2,4]{0,1:T(4,128)(4,1)}, pred[2,4]{0,1:T(4,128)(4,1)S(1)}, u32[]{:S(2)}) copy-start(pred[2,4]{0,1:T(4,128)(4,1)S(1)} %copy.556) | copy-start | bytes 28
  34.0 39.1 %copy-start.38 = (pred[2,4]{0,1:T(4,128)(4,1)}, pred[2,4]{0,1:T(4,128)(4,1)S(1)}, u32[]{:S(2)}) copy-start(pred[2,4]{0,1:T(4,128)(4,1)S(1)} %copy.555) | copy-start | bytes 28
  34.0 36.1 %copy-start.32 = (s32[1024]{0:T(1024)}, s32[1024]{0:T(1024)S(1)}, u32[]{:S(2)}) copy-start(s32[1024]{0:T(1024)S(1)} %pad_clamp_fusion) | copy-start | bytes 12292
  82.6 8.2 copy-start.7
  90.7 3.2 copy-start.12
  94.0 3.4 copy-start.10
  97.4 3.3 copy-start.4
  118.6 258.9 %all-gather.3.cloned.1.call-start = ((), (), s32[]{:S(2)}) async-start(), calls=%async_computation.4 | async-start | bytes 3145728 | tf_op jit(solution)/shard_map/all_gather | solution.py:179
  180.8 3.3 copy-start.31
  184.2 3.9 copy-start.26
  184.2 3.9 copy-start.24
  184.2 5.5 copy-start.28
  202.0 5.1 copy-start.40
  337.4 4.3 copy-start.15
  337.4 5.4 copy-start.18
  342.8 4.6 copy-start.14
  344.2 554.8 %all-reduce.4.cloned.1.call-start = ((), (), s32[]{:S(2)}) async-start(), calls=%async_computation.7 | async-start | bytes 425984 | tf_op jit(solution)/shard_map/psum | solution.py:181
  344.7 3.7 copy-start.16
  350.4 3.9 copy-start.20
  350.9 7.1 copy-start.29
  354.3 4.1 copy-start.27
  377.5 4.1 copy-start.6
  377.5 4.1 copy-start.21
  398.7 526.4 %reduce-scatter.7.cloned.1.call-start = ((), (), s32[]{:S(2)}) async-start(), calls=%async_computation.6 | async-start | bytes 1572864
  408.1 624.0 %all-gather.5.cloned.1.call-start = ((), (), s32[]{:S(2)}) async-start(), calls=%async_computation.5 | async-start | bytes 4259840 | tf_op jit(solution)/shard_map/all_gather | solution.py:184
  930.9 109.6 %copy-start.35 = (pred[2,4]{0,1:T(4,128)(4,1)S(1)}, pred[2,4]{0,1:T(4,128)(4,1)}, u32[]{:S(2)}) copy-start(pred[2,4]{0,1:T(4,128)(4,1)} %copy-done.34) | copy-start | bytes 28
  930.9 109.6 %copy-start.37 = (pred[2,4]{0,1:T(4,128)(4,1)S(1)}, pred[2,4]{0,1:T(4,128)(4,1)}, u32[]{:S(2)}) copy-start(pred[2,4]{0,1:T(4,128)(4,1)} %copy-done.36) | copy-start | bytes 28
  930.9 109.8 %copy-start.39 = (pred[2,4]{0,1:T(4,128)(4,1)S(1)}, pred[2,4]{0,1:T(4,128)(4,1)}, u32[]{:S(2)}) copy-start(pred[2,4]{0,1:T(4,128)(4,1)} %copy-done.38) | copy-start | bytes 28
  (15 other events, 28.3 us)
Sparse Core Ops, SparseCore 0:
  118.7 78.6 reduce-scatter.4
  344.4 33.0 all-gather.2
  398.9 500.1 all-reduce.3
  901.2 23.8 reduce-scatter.6
  926.7 105.3 all-gather.4
